TPU v7x, 32 devices: a whole 2x2x4 slice. The times are simulated.
32 devices in a mesh: ax: 8 (over z, y), az: 4 (over x, core).
Axes of the slice: x: 2, y: 2, z: 4, core: 2. Of those that a mesh axis runs over, the one named last changes fastest.
Arguments:
- density: float32 [32, 256, 256], P('ax', 'az'), may hold values from 0.5 to 2
- velocity: float32 [3, 32, 256, 256], P(None, 'ax', 'az'), may hold values from -12 to 12
Outputs:
- stress_flux: float32 [3, 32, 256, 256], P(None, 'ax', 'az')
- coefficient: float32 [32, 256], P('ax')
All inputs are finite; a program needn't handle non-finite values.
Results may differ from a plain program's by a relative error of at most 0.00002.
Values sent between devices are 32-bit elements; how exact they have to be, the bound alone decides.
A program may use at most 64 MiB of HBM per device.

v0:
```python
import math

import jax
import jax.numpy as jnp
from jax import lax
from jax.sharding import PartitionSpec as P

STEP_AXIAL = 0.5
STEP_RADIAL = 0.25
INNER_RADIUS = 10.0
FILTER_RATIO = 2.0
TINY = 1e-06
COMPONENT_PAIRS = ((0, 0), (1, 1), (2, 2), (0, 1), (0, 2), (1, 2))


def with_halo(block, sides, width, periodic):
    for axis, dim in sides:
        count = lax.axis_size(axis)
        forward = [(i, i + 1) for i in range(count - 1)]
        if periodic:
            forward.append((count - 1, 0))
        backward = [(target, source) for source, target in forward]
        low = lax.ppermute(
            lax.slice_in_dim(block, block.shape[dim] - width, None, axis=dim), axis, forward
        )
        high = lax.ppermute(lax.slice_in_dim(block, 0, width, axis=dim), axis, backward)
        block = jnp.concatenate([low, block, high], axis=dim)
    return block


def trim_cells(values, dim_at, amount):
    extent = values.shape[dim_at]
    return lax.slice_in_dim(values, amount, extent - amount, axis=dim_at)


def interior(values, amount):
    values = trim_cells(values, values.ndim - 3, amount)
    return trim_cells(values, values.ndim - 2, amount)


def pad_radial(values):
    return jnp.concatenate([values[..., :1], values, values[..., -1:]], axis=values.ndim - 1)


def smooth_axis(values, dim_at):
    extent = values.shape[dim_at]
    return (
        0.25 * lax.slice_in_dim(values, 0, extent - 2, axis=dim_at)
        + 0.5 * lax.slice_in_dim(values, 1, extent - 1, axis=dim_at)
        + 0.25 * lax.slice_in_dim(values, 2, extent, axis=dim_at)
    )


def slope_axis(values, dim_at):
    extent = values.shape[dim_at]
    return 0.5 * (
        lax.slice_in_dim(values, 2, extent, axis=dim_at)
        - lax.slice_in_dim(values, 0, extent - 2, axis=dim_at)
    )


def test_filter(values):
    smooth = smooth_axis(values, values.ndim - 3)
    smooth = smooth_axis(smooth, values.ndim - 2)
    return smooth_axis(pad_radial(smooth), values.ndim - 1)


def geometry(radial_cells, azimuth_cells):
    radius = INNER_RADIUS + (jnp.arange(radial_cells, dtype=jnp.float32) + 0.5) * STEP_RADIAL
    angle_step = 2.0 * math.pi / azimuth_cells
    width_sq = (STEP_AXIAL * STEP_RADIAL * angle_step * radius) ** (2.0 / 3.0)
    return (radius, angle_step, width_sq)


def strain(velocity, radius, angle_step):
    d_ax = trim_cells(slope_axis(velocity, 1), 2, 1) / STEP_AXIAL
    d_az = trim_cells(slope_axis(velocity, 2), 1, 1) / (radius * angle_step)
    d_rad = interior(slope_axis(pad_radial(velocity), 3), 1) / STEP_RADIAL
    centre = interior(velocity, 1)
    s_xx = d_ax[0]
    s_rr = d_rad[1]
    s_tt = d_az[2] + centre[1] / radius
    s_xr = 0.5 * (d_rad[0] + d_ax[1])
    s_xt = 0.5 * (d_az[0] + d_ax[2])
    s_rt = 0.5 * (d_az[1] + d_rad[2] - centre[2] / radius)
    strength = jnp.sqrt(
        2.0
        * (
            s_xx * s_xx
            + s_rr * s_rr
            + s_tt * s_tt
            + 2.0 * (s_xr * s_xr + s_xt * s_xt + s_rt * s_rt)
        )
    )
    third = (s_xx + s_rr + s_tt) / 3.0
    deviator = jnp.stack([s_xx - third, s_rr - third, s_tt - third, s_xr, s_xt, s_rt])
    return (deviator, strength)


def model_of(density, width_sq, strength, deviator):
    return density * width_sq * strength * deviator


def pair_products(left_v, right_v):
    return jnp.stack([left_v[first_c] * right_v[second_c] for first_c, second_c in COMPONENT_PAIRS])


def contract(left_t, right_t):
    return (
        left_t[0] * right_t[0]
        + left_t[1] * right_t[1]
        + left_t[2] * right_t[2]
        + 2.0 * (left_t[3] * right_t[3] + left_t[4] * right_t[4] + left_t[5] * right_t[5])
    )


def closure(hat_rho, hat_mom, hat_pairs, hat_model, hat_dev, hat_strength, width_sq):
    mixed_term = (
        FILTER_RATIO * FILTER_RATIO * width_sq * hat_rho * hat_strength * hat_dev - hat_model
    )
    resolved = jnp.stack(
        [hat_mom[first_c] * hat_mom[second_c] / hat_rho for first_c, second_c in COMPONENT_PAIRS]
    )
    leonard = hat_pairs - resolved
    return (contract(leonard, mixed_term), contract(mixed_term, mixed_term))


def lilly_ratio(lm_sum, mm_sum, azimuth_cells):
    return -0.5 * (lm_sum / azimuth_cells) / (mm_sum / azimuth_cells + TINY)


def divergence(stress, radius, angle_step):
    d_ax = trim_cells(slope_axis(stress, 1), 2, 1) / STEP_AXIAL
    d_az = trim_cells(slope_axis(stress, 2), 1, 1) / (radius * angle_step)
    radial_one = pad_radial(jnp.stack([stress[3], stress[1]]) * radius)
    radial_two = pad_radial(stress[5] * (radius * radius))
    d_one = interior(slope_axis(radial_one, 3), 1) / STEP_RADIAL / radius
    d_two = interior(slope_axis(radial_two, 2), 1) / STEP_RADIAL / (radius * radius)
    centre = interior(stress, 1)
    flux_x = d_ax[0] + d_one[0] + d_az[4]
    flux_r = d_ax[3] + d_one[1] + d_az[5] - centre[2] / radius
    flux_t = d_ax[4] + d_two + d_az[2]
    return jnp.stack([flux_x, flux_r, flux_t])


def fix_ends(values, margin, dim_at, is_first, is_last):
    if margin == 0:
        return values
    extent = values.shape[dim_at]
    lower_edge = lax.slice_in_dim(values, margin, margin + 1, axis=dim_at)
    upper_edge = lax.slice_in_dim(values, extent - margin - 1, extent - margin, axis=dim_at)
    view_shape = [1] * values.ndim
    view_shape[dim_at] = extent
    places = jnp.arange(extent).reshape(view_shape)
    values = jnp.where((places < margin) & is_first, lower_edge, values)
    return jnp.where((places >= extent - margin) & is_last, upper_edge, values)


def widen_fields(values, width_cells):
    values = with_halo(values, (("ax", 1),), width_cells, False)
    return with_halo(values, (("az", 2),), width_cells, True)


def widen_stress(stress):
    stress = with_halo(stress, (("ax", 1),), 1, False)
    return with_halo(stress, (("az", 2),), 1, True)


def profile(lm_rows, mm_rows, azimuth_cells):
    lm_sum, mm_sum = lax.psum((lm_rows, mm_rows), "az")
    return lilly_ratio(lm_sum, mm_sum, azimuth_cells)


def shards(density, velocity):
    azimuth_cells = velocity.shape[2] * lax.axis_size("az")
    radius, angle_step, width_sq = geometry(velocity.shape[3], azimuth_cells)
    is_first = lax.axis_index("ax") == 0
    is_last = lax.axis_index("ax") == lax.axis_size("ax") - 1

    def settle(values, margin):
        return fix_ends(values, margin, values.ndim - 3, is_first, is_last)

    margin = 2
    state_wide = widen_fields(jnp.concatenate([density[None], velocity], axis=0), margin)
    state_wide = settle(state_wide, margin)
    rho_wide = state_wide[0]
    vel_wide = state_wide[1:]
    deviator, strength = strain(vel_wide, radius, angle_step)
    deviator = settle(deviator, margin - 1)
    strength = settle(strength, margin - 1)
    model_stress = model_of(interior(rho_wide, 1), width_sq, strength, deviator)
    momentum = rho_wide * vel_wide
    pair_terms = pair_products(momentum, vel_wide)
    hat_rho = settle(test_filter(rho_wide), margin - 1)
    hat_mom = settle(test_filter(momentum), margin - 1)
    hat_pairs = test_filter(interior(pair_terms, 1))
    hat_model = test_filter(model_stress)
    hat_dev, hat_strength = strain(hat_mom / hat_rho, radius, angle_step)
    lm_cells, mm_cells = closure(
        interior(hat_rho, 1),
        interior(hat_mom, 1),
        hat_pairs,
        hat_model,
        hat_dev,
        hat_strength,
        width_sq,
    )
    outer = margin - 2
    lm_rows = jnp.sum(trim_cells(lm_cells, 1, outer), axis=1)
    mm_rows = jnp.sum(trim_cells(mm_cells, 1, outer), axis=1)
    coefficient = profile(lm_rows, mm_rows, azimuth_cells)
    coefficient = fix_ends(coefficient, outer, 0, is_first, is_last)
    stress = -2.0 * coefficient[:, None, :] * interior(model_stress, 1)
    stress = settle(widen_stress(stress), 1)
    stress_flux = divergence(stress, radius, angle_step)
    return (stress_flux, trim_cells(coefficient, 0, outer))


def solution(mesh):
    in_specs = (P("ax", "az", None), P(None, "ax", "az", None))
    out_specs = (P(None, "ax", "az", None), P("ax", None))
    return jax.shard_map(shards, mesh=mesh, in_specs=in_specs, out_specs=out_specs, check_vma=False)
```

profile of v0, /device:TPU:0, one launch (start us, length us, event | category | flops | bytes accessed | tf_op | source)
XLA Modules:
  0.0 90.5 jit_solution(2900627219235501367)
XLA Ops:
  0.6 1.4 %fusion.46 = (f32[4,2,64,256]{3,2,1,0:T(8,128)S(1)}, f32[4,2,64,256]{3,2,1,0:T(8,128)S(1)}) fusion(f32[1,4,64,256]{3,2,1,0:T(8,128)} %bitcast.185, f32[3,4,64,256]{3,2,1,0:T(8,128)} %param.3), kind=kLoop, calls=%fused_computation.100 | loop fusion | flops 262144 | bytes 2097152 | tf_op jit(solution)/shard_map/concatenate | solution.py:184
  2.1 1.3 %collective-permute-start.1 = (f32[4,2,64,256]{3,2,1,0:T(8,128)S(1)}, f32[4,2,64,256]{3,2,1,0:T(8,128)S(1)}, u32[]{:S(2)}, u32[]{:S(2)}) collective-permute-start(f32[4,2,64,256]{3,2,1,0:T(8,128)S(1)} %get-tuple-element.57), channel_id=1, source_target_pairs={{4,0},{8,4},{12,8},{16,12},{20,16},{24,20},{28,24},{5,1},{9,5},{13... | collective-permute-start | bytes 1572872 | tf_op jit(solution)/shard_map/ppermute | solution.py:26
  3.4 5.6 %collective-permute-start = (f32[4,2,64,256]{3,2,1,0:T(8,128)S(1)}, f32[4,2,64,256]{3,2,1,0:T(8,128)S(1)}, u32[]{:S(2)}, u32[]{:S(2)}) collective-permute-start(f32[4,2,64,256]{3,2,1,0:T(8,128)S(1)} %get-tuple-element.56), channel_id=1, source_target_pairs={{0,4},{4,8},{8,12},{12,16},{16,20},{20,24},{24,28},{1,5},{5,9},{9,... | collective-permute-start | bytes 1572872 | tf_op jit(solution)/shard_map/ppermute | solution.py:23
  9.0 9.9 %collective-permute-done.1 = f32[4,2,64,256]{3,2,1,0:T(8,128)S(1)} collective-permute-done((f32[4,2,64,256]{3,2,1,0:T(8,128)S(1)}, f32[4,2,64,256]{3,2,1,0:T(8,128)S(1)}, u32[]{:S(2)}, u32[]{:S(2)}) %collective-permute-start.1) | collective-permute-done | bytes 524320 | tf_op jit(solution)/shard_map/ppermute | solution.py:26
  18.9 11.4 %collective-permute-done = f32[4,2,64,256]{3,2,1,0:T(8,128)S(1)} collective-permute-done((f32[4,2,64,256]{3,2,1,0:T(8,128)S(1)}, f32[4,2,64,256]{3,2,1,0:T(8,128)S(1)}, u32[]{:S(2)}, u32[]{:S(2)}) %collective-permute-start) | collective-permute-done | bytes 524320 | tf_op jit(solution)/shard_map/ppermute | solution.py:23
  30.3 1.2 %collective-permute-start.3 = (f32[4,8,2,256]{3,2,1,0:T(2,128)S(1)}, f32[4,8,2,256]{3,2,1,0:T(2,128)S(1)}, u32[]{:S(2)}, u32[]{:S(2)}) collective-permute-start(f32[4,8,2,256]{3,2,1,0:T(2,128)S(1)} %get-tuple-element.39), channel_id=1, source_target_pairs={{1,0},{2,1},{3,2},{0,3},{5,4},{6,5},{7,6},{4,7},{9,8},{10,9},{11,1... | collective-permute-start | bytes 196616 | tf_op jit(solution)/shard_map/ppermute | solution.py:26
  31.5 2.4 %collective-permute-done.3 = f32[4,8,2,256]{3,2,1,0:T(2,128)S(1)} collective-permute-done((f32[4,8,2,256]{3,2,1,0:T(2,128)S(1)}, f32[4,8,2,256]{3,2,1,0:T(2,128)S(1)}, u32[]{:S(2)}, u32[]{:S(2)}) %collective-permute-start.3) | collective-permute-done | bytes 65568 | tf_op jit(solution)/shard_map/ppermute | solution.py:26
  34.0 1.2 %collective-permute-done.2 = f32[4,8,2,256]{3,2,1,0:T(2,128)S(1)} collective-permute-done((f32[4,8,2,256]{3,2,1,0:T(2,128)S(1)}, f32[4,8,2,256]{3,2,1,0:T(2,128)S(1)}, u32[]{:S(2)}, u32[]{:S(2)}) %collective-permute-start.2) | collective-permute-done | bytes 65568 | tf_op jit(solution)/shard_map/ppermute | solution.py:23
  35.5 0.5 select_select_fusion.1
  37.9 1.0 %fusion.26 = f32[3,6,66,256]{3,2,1,0:T(8,128)S(1)} fusion(f32[3,8,68,1]{3,2,1,0:T(8,128)S(1)} %get-tuple-element.31, f32[3,8,68,256]{3,2,1,0:T(8,128)S(1)} %get-tuple-element.29, f32[3,8,68,1]{3,2,1,0:T(8,128)S(1)} %get-tuple-element.30), kind=kLoop, calls=%fused_computation.52 | loop fusion | flops 1520640 | bytes 2900736 | tf_op jit(solution)/shard_map/div | solution.py:78
  39.0 0.5 fusion.75
  41.1 0.9 %fusion.30 = f32[3,6,66,256]{3,2,1,0:T(8,128)S(1)} fusion(f32[3,6,66,1]{3,2,1,0:T(8,128)S(1)} %get-tuple-element.55, f32[3,6,66,256]{3,2,1,0:T(8,128)S(1)} %fusion.33, f32[3,6,66,1]{3,2,1,0:T(8,128)S(1)} %get-tuple-element.54), kind=kLoop, calls=%fused_computation.59 | loop fusion | flops 2128896 | bytes 2442528 | tf_op jit(solution)/shard_map/add | solution.py:48
  42.6 1.0 %broadcast_divide_fusion = (f32[3,6,66,256]{3,2,1,0:T(8,128)S(1)}, f32[3,6,66,256]{3,2,1,0:T(8,128)S(1)}) fusion(f32[6,66,256]{2,1,0:T(8,128)S(1)} %get-tuple-element.68, f32[3,66,256]{2,1,0:T(8,128)S(1)} %get-tuple-element.53, pred[6]{0:T(512)(128)(4,1)S(1)} %get-tuple-element.72, f32[3,66,256]{2,1,0:T(8,128)S(1)} %get-tuple-element.52, ...), kind=kLoop, calls=%fused_computation.90 | loop fusion | flops 3041280 | bytes 4470060 | tf_op jit(solution)/shard_map/div | solution.py:198
  45.6 0.4 fusion.2
  46.1 0.5 fusion.20
  46.8 0.4 select_multiply_fusion
  47.5 0.6 fusion.13
  48.8 0.6 fusion.41
  50.1 1.1 %fusion.17 = f32[6,4,64,256]{3,2,1,0:T(8,128)S(1)} fusion(f32[6,4,64,256]{3,2,1,0:T(8,128)S(1)} %bitcast_dynamic-update-slice_fusion, f32[6,4,64,1]{3,2,1,0:T(8,128)S(1)} %get-tuple-element.45, f32[6,4,64,256]{3,2,1,0:T(8,128)S(1)} %fusion.20, f32[6,4,64,1]{3,2,1,0:T(8,128)S(1)} %get-tuple-element.44), kind=kLoop, calls=%fused_computation.37 | loop fusion | flops 3145728 | bytes 4730880 | tf_op jit(solution)/shard_map/sub | solution.py:124
  51.2 1.1 %fusion.10 = f32[6,4,64,256]{3,2,1,0:T(8,128)S(1)} fusion(f32[6,4,64,1]{3,2,1,0:T(8,128)S(1)} %get-tuple-element.43, f32[6,4,64,256]{3,2,1,0:T(8,128)S(1)} %fusion.13, f32[6,4,64,1]{3,2,1,0:T(8,128)S(1)} %get-tuple-element.42, f32[6,4,64,256]{3,2,1,0:T(8,128)S(1)} %multiply_dynamic-update-slice_fusion.5, f32[4,64,256]{2,1,0:T(8,128)S(1)} %sqrt_multiply_fusion), kind=kLoop, calls=%fused_computation.25 | loop fusion | flops 3538944 | bytes 4993024 | tf_op jit(solution)/shard_map/sub | solution.py:119
  52.6 6.7 %all-reduce = (f32[4,256]{1,0:T(4,128)S(1)}, f32[4,256]{1,0:T(4,128)S(1)}) all-reduce(f32[4,256]{1,0:T(4,128)S(1)} %get-tuple-element.3, f32[4,256]{1,0:T(4,128)S(1)} %get-tuple-element.2), channel_id=1, replica_groups=mesh['ax'=8,'az'=4] {'az'}, use_global_device_ids=true, to_apply=%region_3.4 | all-reduce | flops 2048 | bytes 16384 | tf_op jit(solution)/shard_map/psum | solution.py:170
  59.3 0.6 broadcast_multiply_fusion.1
  60.2 1.3 %collective-permute-start.5 = (f32[6,1,64,256]{3,2,1,0:T(8,128)S(1)}, f32[6,1,64,256]{3,2,1,0:T(8,128)S(1)}, u32[]{:S(2)}, u32[]{:S(2)}) collective-permute-start(f32[6,1,64,256]{3,2,1,0:T(8,128)S(1)} %get-tuple-element.41), channel_id=1, source_target_pairs={{4,0},{8,4},{12,8},{16,12},{20,16},{24,20},{28,24},{5,1},{9,5},{13... | collective-permute-start | bytes 1179656 | tf_op jit(solution)/shard_map/ppermute | solution.py:26
  61.5 5.0 %collective-permute-start.4 = (f32[6,1,64,256]{3,2,1,0:T(8,128)S(1)}, f32[6,1,64,256]{3,2,1,0:T(8,128)S(1)}, u32[]{:S(2)}, u32[]{:S(2)}) collective-permute-start(f32[6,1,64,256]{3,2,1,0:T(8,128)S(1)} %get-tuple-element.40), channel_id=1, source_target_pairs={{0,4},{4,8},{8,12},{12,16},{16,20},{20,24},{24,28},{1,5},{5,9},{9,... | collective-permute-start | bytes 1179656 | tf_op jit(solution)/shard_map/ppermute | solution.py:23
  66.5 6.2 %collective-permute-done.5 = f32[6,1,64,256]{3,2,1,0:T(8,128)S(1)} collective-permute-done((f32[6,1,64,256]{3,2,1,0:T(8,128)S(1)}, f32[6,1,64,256]{3,2,1,0:T(8,128)S(1)}, u32[]{:S(2)}, u32[]{:S(2)}) %collective-permute-start.5) | collective-permute-done | bytes 393248 | tf_op jit(solution)/shard_map/ppermute | solution.py:26
  72.8 8.6 %collective-permute-done.4 = f32[6,1,64,256]{3,2,1,0:T(8,128)S(1)} collective-permute-done((f32[6,1,64,256]{3,2,1,0:T(8,128)S(1)}, f32[6,1,64,256]{3,2,1,0:T(8,128)S(1)}, u32[]{:S(2)}, u32[]{:S(2)}) %collective-permute-start.4) | collective-permute-done | bytes 393248 | tf_op jit(solution)/shard_map/ppermute | solution.py:23
  81.4 0.9 collective-permute-start.7
  82.3 1.6 %collective-permute-done.7 = f32[6,6,1,256]{3,2,1,0:T(1,128)S(1)} collective-permute-done((f32[6,6,1,256]{3,2,1,0:T(1,128)S(1)}, f32[6,6,1,256]{3,2,1,0:T(1,128)S(1)}, u32[]{:S(2)}, u32[]{:S(2)}) %collective-permute-start.7) | collective-permute-done | bytes 36896 | tf_op jit(solution)/shard_map/ppermute | solution.py:26
  83.9 1.7 %collective-permute-done.6 = f32[6,6,1,256]{3,2,1,0:T(1,128)S(1)} collective-permute-done((f32[6,6,1,256]{3,2,1,0:T(1,128)S(1)}, f32[6,6,1,256]{3,2,1,0:T(1,128)S(1)}, u32[]{:S(2)}, u32[]{:S(2)}) %collective-permute-start.6) | collective-permute-done | bytes 36896 | tf_op jit(solution)/shard_map/ppermute | solution.py:23
  86.1 0.5 select_select_fusion
  86.6 0.6 fusion.110
  89.5 0.9 %pad_maximum_fusion.12 = f32[3,4,64,256]{3,2,1,0:T(8,128)} fusion(f32[1,4,64,256]{3,2,1,0:T(8,128)S(1)} %fusion.77, f32[1,4,64,256]{3,2,1,0:T(8,128)S(1)} %get-tuple-element.15, f32[1,4,64,256]{3,2,1,0:T(8,128)S(1)} %get-tuple-element.14), kind=kLoop, calls=%fused_computation.89 | loop fusion | flops 393216 | bytes 1572864 | tf_op jit(solution)/shard_map/stack | solution.py:143
  (86 shorter events, 11.5 us)
Async XLA Ops:
  0.6 29.7 %copy-start.1 = (f32[4,64,256]{2,1,0:T(8,128)S(1)}, f32[4,64,256]{2,1,0:T(8,128)}, u32[]{:S(2)}) copy-start(f32[4,64,256]{2,1,0:T(8,128)} %param.2) | copy-start | bytes 786436
  0.6 29.6 %copy-start = (f32[3,4,64,256]{3,2,1,0:T(8,128)S(1)}, f32[3,4,64,256]{3,2,1,0:T(8,128)}, u32[]{:S(2)}) copy-start(f32[3,4,64,256]{3,2,1,0:T(8,128)} %param.3) | copy-start | bytes 2359300
  2.1 16.8 %collective-permute-start.1 = (f32[4,2,64,256]{3,2,1,0:T(8,128)S(1)}, f32[4,2,64,256]{3,2,1,0:T(8,128)S(1)}, u32[]{:S(2)}, u32[]{:S(2)}) collective-permute-start(f32[4,2,64,256]{3,2,1,0:T(8,128)S(1)} %get-tuple-element.57), channel_id=1, source_target_pairs={{4,0},{8,4},{12,8},{16,12},{20,16},{24,20},{28,24},{5,1},{9,5},{13... | collective-permute-start | bytes 1572872 | tf_op jit(solution)/shard_map/ppermute | solution.py:26
  3.4 26.9 %collective-permute-start = (f32[4,2,64,256]{3,2,1,0:T(8,128)S(1)}, f32[4,2,64,256]{3,2,1,0:T(8,128)S(1)}, u32[]{:S(2)}, u32[]{:S(2)}) collective-permute-start(f32[4,2,64,256]{3,2,1,0:T(8,128)S(1)} %get-tuple-element.56), channel_id=1, source_target_pairs={{0,4},{4,8},{8,12},{12,16},{16,20},{20,24},{24,28},{1,5},{5,9},{9,... | collective-permute-start | bytes 1572872 | tf_op jit(solution)/shard_map/ppermute | solution.py:23
  30.3 3.6 %collective-permute-start.3 = (f32[4,8,2,256]{3,2,1,0:T(2,128)S(1)}, f32[4,8,2,256]{3,2,1,0:T(2,128)S(1)}, u32[]{:S(2)}, u32[]{:S(2)}) collective-permute-start(f32[4,8,2,256]{3,2,1,0:T(2,128)S(1)} %get-tuple-element.39), channel_id=1, source_target_pairs={{1,0},{2,1},{3,2},{0,3},{5,4},{6,5},{7,6},{4,7},{9,8},{10,9},{11,1... | collective-permute-start | bytes 196616 | tf_op jit(solution)/shard_map/ppermute | solution.py:26
  31.5 3.7 %collective-permute-start.2 = (f32[4,8,2,256]{3,2,1,0:T(2,128)S(1)}, f32[4,8,2,256]{3,2,1,0:T(2,128)S(1)}, u32[]{:S(2)}, u32[]{:S(2)}) collective-permute-start(f32[4,8,2,256]{3,2,1,0:T(2,128)S(1)} %get-tuple-element.38), channel_id=1, source_target_pairs={{0,1},{1,2},{2,3},{3,0},{4,5},{5,6},{6,7},{7,4},{8,9},{9,10},{10,1... | collective-permute-start | bytes 196616 | tf_op jit(solution)/shard_map/ppermute | solution.py:23
  60.2 12.6 %collective-permute-start.5 = (f32[6,1,64,256]{3,2,1,0:T(8,128)S(1)}, f32[6,1,64,256]{3,2,1,0:T(8,128)S(1)}, u32[]{:S(2)}, u32[]{:S(2)}) collective-permute-start(f32[6,1,64,256]{3,2,1,0:T(8,128)S(1)} %get-tuple-element.41), channel_id=1, source_target_pairs={{4,0},{8,4},{12,8},{16,12},{20,16},{24,20},{28,24},{5,1},{9,5},{13... | collective-permute-start | bytes 1179656 | tf_op jit(solution)/shard_map/ppermute | solution.py:26
  61.5 19.9 %collective-permute-start.4 = (f32[6,1,64,256]{3,2,1,0:T(8,128)S(1)}, f32[6,1,64,256]{3,2,1,0:T(8,128)S(1)}, u32[]{:S(2)}, u32[]{:S(2)}) collective-permute-start(f32[6,1,64,256]{3,2,1,0:T(8,128)S(1)} %get-tuple-element.40), channel_id=1, source_target_pairs={{0,4},{4,8},{8,12},{12,16},{16,20},{20,24},{24,28},{1,5},{5,9},{9,... | collective-permute-start | bytes 1179656 | tf_op jit(solution)/shard_map/ppermute | solution.py:23
  81.4 2.5 %collective-permute-start.7 = (f32[6,6,1,256]{3,2,1,0:T(1,128)S(1)}, f32[6,6,1,256]{3,2,1,0:T(1,128)S(1)}, u32[]{:S(2)}, u32[]{:S(2)}) collective-permute-start(f32[6,6,1,256]{3,2,1,0:T(1,128)S(1)} %get-tuple-element.27), channel_id=1, source_target_pairs={{1,0},{2,1},{3,2},{0,3},{5,4},{6,5},{7,6},{4,7},{9,8},{10,9},{11,1... | collective-permute-start | bytes 110600 | tf_op jit(solution)/shard_map/ppermute | solution.py:26
  82.3 3.4 %collective-permute-start.6 = (f32[6,6,1,256]{3,2,1,0:T(1,128)S(1)}, f32[6,6,1,256]{3,2,1,0:T(1,128)S(1)}, u32[]{:S(2)}, u32[]{:S(2)}) collective-permute-start(f32[6,6,1,256]{3,2,1,0:T(1,128)S(1)} %get-tuple-element.26), channel_id=1, source_target_pairs={{0,1},{1,2},{2,3},{3,0},{4,5},{5,6},{6,7},{7,4},{8,9},{9,10},{10,1... | collective-permute-start | bytes 110600 | tf_op jit(solution)/shard_map/ppermute | solution.py:23
where the time goes:
time: 90.7 us; the launch traced here: 90.5 us
  waiting for transfers between devices  43.1 us (48%)
  other arithmetic  19.9 us (22%)
  starting transfers between devices  15.2 us (17%)
  blocking collectives  6.68 us (7%)
  local copies, waits for them, and re-layouts  4.23 us (5%)
  between operations  1.31 us (1%)
    ppermute x4, waiting for transfers between devices, with_halo(): lax.ppermute(lax.slice_in_dim(block, block.shape[dim] - width, None, axis...  22.9 us
    ppermute x4, waiting for transfers between devices, with_halo(): lax.ppermute(lax.slice_in_dim(block, 0, width, axis=dim), axis, backward)  20.1 us
    ppermute x4, starting transfers between devices, with_halo(): lax.ppermute(lax.slice_in_dim(block, block.shape[dim] - width, None, axis...  10.6 us
    psum x1, blocking collectives, profile(): lm_sum, mm_sum = lax.psum((lm_rows, mm_rows), 'az')  6.68 us
    ppermute x4, starting transfers between devices, with_halo(): lax.ppermute(lax.slice_in_dim(block, 0, width, axis=dim), axis, backward)  4.63 us
    add x10, other arithmetic, smooth_axis(): 0.25 * lax.slice_in_dim(values, 0, extent - 2, axis=dim_at)  3.88 us
    slice x6, local copies, waits for them, and re-layouts, slope_axis(): lax.slice_in_dim(values, 2, extent, axis=dim_at)  2.03 us
  transfers between devices with their start and end apart: 8, of which 8 were waited for; matrix products, arithmetic and copies ran while one was open for 0% of the time, Pallas kernels for 0%

commit v1 on v0

v1 whole, which is shorter than its diff:
```python
import functools
import math

import jax
import jax.numpy as jnp
import numpy as np
from jax import lax
from jax.experimental import pallas as pl
from jax.experimental.pallas import tpu as pltpu
from jax.sharding import PartitionSpec as P

STEP_AXIAL = 0.5
STEP_RADIAL = 0.25
INNER_RADIUS = 10.0
FILTER_RATIO = 2.0
TINY = 1e-06
PAIRS = ((0, 0), (1, 1), (2, 2), (0, 1), (0, 2), (1, 2))
LANES = 128
SUB = 8
EDGE = 16
MESH_ID = pl.DeviceIdType.MESH


def geometry(radial, azimuth_cells):
    radius = INNER_RADIUS + (np.arange(radial, dtype=np.float64) + 0.5) * STEP_RADIAL
    angle = 2.0 * math.pi / azimuth_cells
    width = (STEP_AXIAL * STEP_RADIAL * angle * radius) ** (2.0 / 3.0)
    rows = np.stack(
        [
            1.0 / radius,
            0.5 / (radius * angle),
            width,
            FILTER_RATIO**2 * width,
            radius,
            0.5 / STEP_RADIAL / radius,
            radius * radius,
            0.5 / STEP_RADIAL / (radius * radius),
        ]
    ).astype(np.float32)
    rows = rows.reshape(rows.shape[0], radial // LANES, 1, LANES)
    return np.ascontiguousarray(np.broadcast_to(rows, rows.shape[:2] + (SUB, LANES)))


def before(x):
    lane = lax.broadcasted_iota(jnp.int32, x.shape, x.ndim - 1)
    y = pltpu.roll(x, 1, x.ndim - 1)
    fill = jnp.concatenate([x[:1], y[:-1]], axis=0)
    return jnp.where(lane == 0, fill, y)


def after(x):
    lane = lax.broadcasted_iota(jnp.int32, x.shape, x.ndim - 1)
    y = pltpu.roll(x, LANES - 1, x.ndim - 1)
    fill = jnp.concatenate([y[1:], x[-1:]], axis=0)
    return jnp.where(lane == LANES - 1, fill, y)


def rise(x):
    return after(x) - before(x)


def strain(dx, dr, dt, ur, ut, inv_r):
    s_xx, s_rr = dx[0], dr[1]
    s_tt = dt[2] + ur * inv_r
    s_xr = 0.5 * (dr[0] + dx[1])
    s_xt = 0.5 * (dt[0] + dx[2])
    s_rt = 0.5 * (dt[1] + dr[2] - ut * inv_r)
    size = jnp.sqrt(
        2.0
        * (
            s_xx * s_xx
            + s_rr * s_rr
            + s_tt * s_tt
            + 2.0 * (s_xr * s_xr + s_xt * s_xt + s_rt * s_rt)
        )
    )
    third = (s_xx + s_rr + s_tt) * (1.0 / 3.0)
    return (s_xx - third, s_rr - third, s_tt - third, s_xr, s_xt, s_rt), size


def kernel(
    n_ax, n_az, nx, nt, nh,
    rho_ref, vel_ref, geo_ref, flux_ref, coef_ref,
    S, M, H, V, HM, PX, MX, ACC, part, rec, rec_lo, rec_hi, CS,
    own_sem, halo_send, halo_recv, corner_send, corner_recv, sum_send, sum_recv,
):
    me_ax, me_az = lax.axis_index("ax"), lax.axis_index("az")
    left, right = lax.rem(me_az + n_az - 1, n_az), lax.rem(me_az + 1, n_az)
    has_lo, has_hi = me_ax > 0, me_ax < n_ax - 1
    azimuth_cells = nt * n_az

    own = []
    for h in range(nh):
        lanes = pl.ds(h * LANES, LANES)
        cols = pl.ds(EDGE, nt)
        own.append(pltpu.make_async_copy(
            rho_ref.at[:, :, lanes], S.at[0, pl.ds(2, nx), h, cols, :], own_sem.at[2 * h]))
        own.append(pltpu.make_async_copy(
            vel_ref.at[:, :, :, lanes], S.at[pl.ds(1, 3), pl.ds(2, nx), h, cols, :], own_sem.at[2 * h + 1]))
    for c in own:
        c.start()

    barrier = pltpu.get_barrier_semaphore()

    def greet(ax, az):
        pl.semaphore_signal(barrier, inc=1, device_id=(ax, az), device_id_type=MESH_ID)

    for d in range(1, n_az):
        greet(me_ax, lax.rem(me_az + d, n_az))

    @pl.when(has_lo)
    def _():
        for d in range(n_az):
            greet(me_ax - 1, lax.rem(me_az + d, n_az))

    @pl.when(has_hi)
    def _():
        for d in range(n_az):
            greet(me_ax + 1, lax.rem(me_az + d, n_az))

    peers = n_az - 1 + jnp.where(has_lo, n_az, 0) + jnp.where(has_hi, n_az, 0)
    pl.semaphore_wait(barrier, peers)

    def halo(kind, src_rows, src_cols, dst_rows, dst_cols, target):
        copies = []
        for h in range(nh):
            lanes = pl.ds(h * LANES, LANES)
            copies.append(pltpu.make_async_remote_copy(
                src_ref=rho_ref.at[src_rows, src_cols, lanes],
                dst_ref=S.at[0, dst_rows, h, dst_cols, :],
                send_sem=halo_send.at[kind, 2 * h], recv_sem=halo_recv.at[kind, 2 * h],
                device_id=target, device_id_type=MESH_ID))
            copies.append(pltpu.make_async_remote_copy(
                src_ref=vel_ref.at[:, src_rows, src_cols, lanes],
                dst_ref=S.at[pl.ds(1, 3), dst_rows, h, dst_cols, :],
                send_sem=halo_send.at[kind, 2 * h + 1], recv_sem=halo_recv.at[kind, 2 * h + 1],
                device_id=target, device_id_type=MESH_ID))
        return copies

    every = pl.ds(0, nt)
    mid = pl.ds(EDGE, nt)
    up = [halo(0, pl.ds(nx - 1, 1), every, pl.ds(1, 1), mid, (me_ax + 1, me_az)),
          halo(1, pl.ds(nx - 2, 1), every, pl.ds(0, 1), mid, (me_ax + 1, me_az))]
    down = [halo(2, pl.ds(0, 1), every, pl.ds(nx + 2, 1), mid, (me_ax - 1, me_az)),
            halo(3, pl.ds(1, 1), every, pl.ds(nx + 3, 1), mid, (me_ax - 1, me_az))]
    around = halo(4, pl.ds(0, nx), pl.ds(nt - SUB, SUB), pl.ds(2, nx), pl.ds(EDGE - SUB, SUB), (me_ax, right))
    around += halo(5, pl.ds(0, nx), pl.ds(0, SUB), pl.ds(2, nx), pl.ds(EDGE + nt, SUB), (me_ax, left))

    for c in around:
        c.start()
    for step in range(2):
        @pl.when(has_hi)
        def _():
            for c in up[step]:
                c.start()

        @pl.when(has_lo)
        def _():
            for c in down[step]:
                c.start()

    def corner(slot, row):
        return [
            pltpu.make_async_remote_copy(
                src_ref=S.at[:, row, :, pl.ds(EDGE + nt - SUB, SUB), :],
                dst_ref=S.at[:, row, :, pl.ds(EDGE - SUB, SUB), :],
                send_sem=corner_send.at[slot, 0], recv_sem=corner_recv.at[slot, 0],
                device_id=(me_ax, right), device_id_type=MESH_ID),
            pltpu.make_async_remote_copy(
                src_ref=S.at[:, row, :, pl.ds(EDGE, SUB), :],
                dst_ref=S.at[:, row, :, pl.ds(EDGE + nt, SUB), :],
                send_sem=corner_send.at[slot, 1], recv_sem=corner_recv.at[slot, 1],
                device_id=(me_ax, left), device_id_type=MESH_ID),
        ]

    def receive(step):
        lo_corner, hi_corner = corner(step, 1 - step), corner(2 + step, nx + 2 + step)

        @pl.when(has_lo)
        def _():
            for c in up[step]:
                c.wait_recv()
            for c in lo_corner:
                c.start()

        @pl.when(has_hi)
        def _():
            for c in down[step]:
                c.wait_recv()
            for c in hi_corner:
                c.start()

        @pl.when(has_lo)
        def _():
            for c in lo_corner:
                c.wait()

        @pl.when(has_hi)
        def _():
            for c in hi_corner:
                c.wait()

    def low(r):
        return jnp.maximum(r - 1, jnp.where(has_lo, -2, 0))

    def high(r):
        return jnp.minimum(r + 1, jnp.where(has_hi, nx + 1, nx - 1))

    def sweep(first, stride, count, tiles, body):
        def step(at, carry):
            r = first + stride * (at // tiles)
            body(r, lax.rem(at, tiles))
            return carry

        lax.fori_loop(0, count * tiles, step, 0)

    wide = nt // SUB + 2

    def near(ref, lead, row, col, shift):
        return ref[lead, row, :, pl.ds(col + shift, SUB), :]

    def tile(ref, lead, row, col):
        return ref[lead, row, :, pl.ds(pl.multiple_of(col, SUB), SUB), :]

    def put(ref, lead, row, col, value):
        ref[lead, row, :, pl.ds(pl.multiple_of(col, SUB), SUB), :] = value

    def first_pass(with_pairs):
        def body(r, t):
            c = (EDGE - SUB) + t * SUB
            rows = (low(r) + 2, r + 2, high(r) + 2)
            rho = [tile(S, 0, q, c) for q in rows]
            vel = [[tile(S, 1 + a, q, c) for a in range(3)] for q in rows]
            inv_r, az_scale, width = geo_ref[0], geo_ref[1], geo_ref[2]
            dx = [vel[2][a] - vel[0][a] for a in range(3)]
            dr = [rise(vel[1][a]) * (0.5 / STEP_RADIAL) for a in range(3)]
            dt = [(near(S, 1 + a, r + 2, c, 1) - near(S, 1 + a, r + 2, c, -1)) * az_scale for a in range(3)]
            dev, size = strain(dx, dr, dt, vel[1][1], vel[1][2], inv_r)
            scale = rho[1] * width * size
            for a in range(6):
                put(M, a, r + 1, c, scale * dev[a])
            mom = [[rho[q] * vel[q][a] for a in range(3)] for q in range(3)]
            put(H, 0, r + 1, c, (rho[0] + rho[1]) + (rho[1] + rho[2]))
            for a in range(3):
                put(H, 1 + a, r + 1, c, (mom[0][a] + mom[1][a]) + (mom[1][a] + mom[2][a]))
            if with_pairs:
                for at, (a, b) in enumerate(PAIRS):
                    p = [mom[q][a] * vel[q][b] for q in range(3)]
                    put(PX, at, r, c, (p[0] + p[1]) + (p[1] + p[2]))
        return body

    def smooth(ref, lead, row, c):
        mid_value = tile(ref, lead, row, c)
        s = (near(ref, lead, row, c, -1) + near(ref, lead, row, c, 1)) + (mid_value + mid_value)
        return ((before(s) + after(s)) + (s + s)) * (1.0 / 64.0)

    def hat_pass(r, t):
        c = (EDGE - SUB) + t * SUB
        hat = [smooth(H, a, r + 1, c) for a in range(4)]
        inv = 1.0 / hat[0]
        for a in range(4):
            put(HM, a, r + 1, c, hat[a])
        for a in range(3):
            put(V, a, r + 1, c, hat[1 + a] * inv)

    def model_pass(r, t):
        c = (EDGE - SUB) + t * SUB
        for a in range(6):
            m = tile(M, a, r + 1, c)
            put(MX, a, r, c, (tile(M, a, low(r) + 1, c) + m) + (m + tile(M, a, high(r) + 1, c)))

    def closure_pass(r, t):
        c = EDGE + t * SUB
        inv_r, az_scale, width4 = geo_ref[0], geo_ref[1], geo_ref[3]
        hv = [tile(V, a, r + 1, c) for a in range(3)]
        dx = [tile(V, a, high(r) + 1, c) - tile(V, a, low(r) + 1, c) for a in range(3)]
        dr = [rise(hv[a]) * (0.5 / STEP_RADIAL) for a in range(3)]
        dt = [(near(V, a, r + 1, c, 1) - near(V, a, r + 1, c, -1)) * az_scale for a in range(3)]
        dev, size = strain(dx, dr, dt, hv[1], hv[2], inv_r)
        scale = width4 * tile(HM, 0, r + 1, c) * size
        hm = [tile(HM, 1 + a, r + 1, c) for a in range(3)]
        lm, mm = [], []
        for at, (a, b) in enumerate(PAIRS):
            mixed = scale * dev[at] - smooth(MX, at, r, c)
            leonard = smooth(PX, at, r, c) - hm[a] * hv[b]
            lm.append(leonard * mixed)
            mm.append(mixed * mixed)
        ACC[r, 0] += (lm[0] + lm[1] + lm[2]) + 2.0 * (lm[3] + lm[4] + lm[5])
        ACC[r, 1] += (mm[0] + mm[1] + mm[2]) + 2.0 * (mm[3] + mm[4] + mm[5])

    ACC[...] = jnp.zeros_like(ACC)
    for c in own:
        c.wait()
    for c in around:
        c.wait_recv()
    sweep(1, 1, nx - 2, wide, first_pass(True))
    sweep(1, 1, nx - 2, wide, hat_pass)
    receive(0)
    sweep(0, nx - 1, 2, wide, first_pass(True))
    sweep(0, nx - 1, 2, wide, hat_pass)
    sweep(1, 1, nx - 2, wide, model_pass)
    sweep(1, 1, nx - 2, nt // SUB, closure_pass)
    receive(1)
    sweep(-1, nx + 1, 2, wide, first_pass(False))
    sweep(-1, nx + 1, 2, wide, hat_pass)
    sweep(0, nx - 1, 2, wide, model_pass)
    sweep(0, nx - 1, 2, nt // SUB, closure_pass)

    for r in range(nx):
        for q in range(2):
            for h in range(nh):
                row = jnp.sum(ACC[r, q, h], axis=0, keepdims=True)
                part[r, pl.ds(q * nh + h, 1), :] = row
                rec[me_az, r, pl.ds(q * nh + h, 1), :] = row

    def share(kind, d, src, dst, ax):
        return pltpu.make_async_remote_copy(
            src_ref=src, dst_ref=dst.at[me_az],
            send_sem=sum_send.at[kind, d], recv_sem=sum_recv.at[kind, d],
            device_id=(ax, lax.rem(me_az + d, n_az)), device_id_type=MESH_ID)

    to_hi = [share(1, d, part.at[nx - 1], rec_lo, me_ax + 1) for d in range(n_az)]
    to_lo = [share(2, d, part.at[0], rec_hi, me_ax - 1) for d in range(n_az)]
    across = [share(0, d, part, rec, me_ax) for d in range(1, n_az)]

    @pl.when(has_hi)
    def _():
        for c in to_hi:
            c.start()

    @pl.when(has_lo)
    def _():
        for c in to_lo:
            c.start()

    for c in across:
        c.start()

    def ratio(sums):
        lm, mm = sums[:nh], sums[nh:]
        return -0.5 * (lm * (1.0 / azimuth_cells)) / (mm * (1.0 / azimuth_cells) + TINY)

    def total(ref):
        sums = ref[0]
        for d in range(1, n_az):
            sums = sums + ref[d]
        return sums

    def keep(row, value):
        for h in range(nh):
            CS[row, h] = jnp.broadcast_to(-2.0 * value[h:h + 1], (SUB, LANES))

    for c in across:
        c.wait_recv()
    for r in range(nx):
        value = ratio(total(rec.at[:, r]))
        keep(r + 1, value)
        for h in range(nh):
            coef_ref[pl.ds(r, 1), pl.ds(h * LANES, LANES)] = value[h:h + 1]

    def flux_pass(r, t):
        c = EDGE + t * SUB
        inv_r, az_scale = geo_ref[0], geo_ref[1]
        radius, back, radius2, back2 = geo_ref[4], geo_ref[5], geo_ref[6], geo_ref[7]
        lo, hi = low(r) + 1, high(r) + 1
        here, below, above = CS[r + 1], CS[lo], CS[hi]

        def axial(a):
            return above * tile(M, a, hi, c) - below * tile(M, a, lo, c)

        def around_of(a):
            return (near(M, a, r + 1, c, 1) - near(M, a, r + 1, c, -1)) * turn

        turn = here * az_scale
        once = here * radius
        d_xr = rise(once * tile(M, 3, r + 1, c)) * back
        d_rr = rise(once * tile(M, 1, r + 1, c)) * back
        d_rt = rise(here * radius2 * tile(M, 5, r + 1, c)) * back2
        out = (
            axial(0) + d_xr + around_of(4),
            axial(3) + d_rr + around_of(5) - here * tile(M, 2, r + 1, c) * inv_r,
            axial(4) + d_rt + around_of(2),
        )
        rows = pl.ds(pl.multiple_of(t * SUB, SUB), SUB)
        for a in range(3):
            for h in range(nh):
                flux_ref[a, r, rows, pl.ds(h * LANES, LANES)] = out[a][h]

    sweep(1, 1, nx - 2, nt // SUB, flux_pass)

    @pl.when(has_lo)
    def _():
        for c in to_hi:
            c.wait_recv()
        keep(0, ratio(total(rec_lo)))

    @pl.when(has_hi)
    def _():
        for c in to_lo:
            c.wait_recv()
        keep(nx + 1, ratio(total(rec_hi)))

    sweep(0, nx - 1, 2, nt // SUB, flux_pass)

    for c in across + around:
        c.wait_send()

    @pl.when(has_hi)
    def _():
        for c in up[0] + up[1] + to_hi:
            c.wait_send()

    @pl.when(has_lo)
    def _():
        for c in down[0] + down[1] + to_lo:
            c.wait_send()


def shards(n_ax, n_az, density, velocity):
    nx, nt, radial = density.shape
    nh = radial // LANES
    cols = nt + 2 * EDGE
    geo = jnp.asarray(geometry(radial, nt * n_az))

    def field(count, rows):
        return pltpu.VMEM((count, rows, nh, cols, LANES), jnp.float32)

    dma = pltpu.SemaphoreType.DMA
    return pl.pallas_call(
        functools.partial(kernel, n_ax, n_az, nx, nt, nh),
        out_shape=(
            jax.ShapeDtypeStruct(velocity.shape, jnp.float32),
            jax.ShapeDtypeStruct((nx, radial), jnp.float32),
        ),
        in_specs=[
            pl.BlockSpec(memory_space=pl.ANY),
            pl.BlockSpec(memory_space=pl.ANY),
            pl.BlockSpec(memory_space=pltpu.VMEM),
        ],
        out_specs=(
            pl.BlockSpec(memory_space=pltpu.VMEM),
            pl.BlockSpec(memory_space=pltpu.VMEM),
        ),
        scratch_shapes=[
            field(4, nx + 4),
            field(6, nx + 2),
            field(4, nx + 2),
            field(3, nx + 2),
            field(4, nx + 2),
            field(6, nx),
            field(6, nx),
            pltpu.VMEM((nx, 2, nh, SUB, LANES), jnp.float32),
            pltpu.VMEM((nx, 2 * nh, LANES), jnp.float32),
            pltpu.VMEM((n_az, nx, 2 * nh, LANES), jnp.float32),
            pltpu.VMEM((n_az, 2 * nh, LANES), jnp.float32),
            pltpu.VMEM((n_az, 2 * nh, LANES), jnp.float32),
            pltpu.VMEM((nx + 2, nh, SUB, LANES), jnp.float32),
            dma((2 * nh,)),
            dma((6, 2 * nh)),
            dma((6, 2 * nh)),
            dma((4, 2)),
            dma((4, 2)),
            dma((3, n_az)),
            dma((3, n_az)),
        ],
        compiler_params=pltpu.CompilerParams(collective_id=0, has_side_effects=True),
        name="closure",
    )(density, velocity, geo)


def solution(mesh):
    in_specs = (P("ax", "az", None), P(None, "ax", "az", None))
    out_specs = (P(None, "ax", "az", None), P("ax", None))
    body = functools.partial(shards, mesh.shape["ax"], mesh.shape["az"])
    return jax.shard_map(body, mesh=mesh, in_specs=in_specs, out_specs=out_specs, check_vma=False)
```

time: 90.7 us -> 54 us (0.60)
  Pallas kernels: 0 us -> 50.5 us
  waiting for transfers between devices: 43.1 us -> 0 us
  other arithmetic: 19.9 us -> 0 us
  starting transfers between devices: 15.2 us -> 0 us
  blocking collectives: 6.68 us -> 0 us
  local copies, waits for them, and re-layouts: 4.23 us -> 2.66 us
    pallas_call x0 -> x1, Pallas kernels: none -> 50.5 us  [shards(): pl.pallas_call(functools.partial(kernel, n_ax, n_az, nx, nt, nh), out_sha...]
    ppermute x8 -> x0, waiting for transfers between devices: 43.1 us -> none  [the longest x4 22.9 us: with_halo(): lax.ppermute(lax.slice_in_dim(block, block.shape[dim] - width, None, axis...]
    ppermute x8 -> x0, starting transfers between devices: 15.2 us -> none  [the longest x4 10.6 us: with_halo(): lax.ppermute(lax.slice_in_dim(block, block.shape[dim] - width, None, axis...]
    psum x1 -> x0, blocking collectives: 6.68 us -> none  [profile(): lm_sum, mm_sum = lax.psum((lm_rows, mm_rows), 'az')]
    div x10 -> x0, other arithmetic: 4.37 us -> none  [the longest x2 1.57 us: strain(): d_rad = interior(slope_axis(pad_radial(velocity), 3), 1) / STEP_RADIAL]
    add x12 -> x0, other arithmetic: 4.04 us -> none  [the longest x10 3.88 us: smooth_axis(): 0.25 * lax.slice_in_dim(values, 0, extent - 2, axis=dim_at)]
    slice x17 -> x0, local copies, waits for them, and re-layouts: 3.95 us -> none  [the longest x6 2.03 us: slope_axis(): lax.slice_in_dim(values, 2, extent, axis=dim_at)]
    unnamed x4, local copies, waits for them, and re-layouts: 0.01 us -> 2.66 us
  transfers between devices with their start and end apart: 8 -> 0, of which waited for: 8 -> 0; matrix products, arithmetic and copies ran while one was open for 0% -> 0% of each run, Pallas kernels for 0% -> 0%
where the time goes in v1:
time: 54 us; the launch traced here: 53.8 us
  Pallas kernels  50.5 us (94%)
  local copies, waits for them, and re-layouts  2.66 us (5%)
  between operations  0.65 us (1%)
    pallas_call x1, Pallas kernels, shards(): pl.pallas_call(functools.partial(kernel, n_ax, n_az, nx, nt, nh), out_sha...  50.5 us
    unnamed x4, local copies, waits for them, and re-layouts  2.66 us

profile of v1, /device:TPU:0, one launch (start us, length us, event | category | flops | bytes accessed | tf_op | source)
XLA Modules:
  0.0 53.8 jit_solution(8654628102856507378)
XLA Ops:
  0.6 50.5 %closure.1 = (f32[3,4,64,256]{3,2,1,0:T(8,128)}, f32[4,256]{1,0:T(4,128)}) custom-call(f32[4,64,256]{2,1,0:T(8,128)} %rho_ref.1, f32[3,4,64,256]{3,2,1,0:T(8,128)} %vel_ref.1, f32[8,2,8,128]{3,2,1,0:T(8,128)} %constant.2.clone.geo_ref), custom_call_target="tpu_custom_call" | custom-call | tf_op jit(solution)/shard_map/closure/pallas_call | solution.py:429
  51.2 0.0 copy-start
  51.2 2.1 %copy.7 = f32[3,4,64,256]{3,2,1,0:T(8,128)} copy(f32[3,4,64,256]{3,2,1,0:T(8,128)} %get-tuple-element.4) | data formatting | bytes 1572864
  53.2 0.0 copy-done
  53.2 0.6 %copy.8 = f32[4,256]{1,0:T(4,128)} copy(f32[4,256]{1,0:T(4,128)S(1)} %copy-done) | data formatting | bytes 8192
Async XLA Ops:
  51.2 2.1 %copy-start = (f32[4,256]{1,0:T(4,128)S(1)}, f32[4,256]{1,0:T(4,128)}, u32[]{:S(2)}) copy-start(f32[4,256]{1,0:T(4,128)} %get-tuple-element.5) | copy-start | bytes 12292

commit v2 on v1

--- a/solution.py
+++ b/solution.py
@@ -17,6 +17,7 @@
 PAIRS = ((0, 0), (1, 1), (2, 2), (0, 1), (0, 2), (1, 2))
 LANES = 128
 SUB = 8
+BLOCKS = {"first": 5, "hat": 10, "model": 10, "closure": 4, "flux": 4}
 EDGE = 16
 MESH_ID = pl.DeviceIdType.MESH
 
@@ -137,18 +138,25 @@
                 device_id=target, device_id_type=MESH_ID))
         return copies
 
-    every = pl.ds(0, nt)
-    mid = pl.ds(EDGE, nt)
-    up = [halo(0, pl.ds(nx - 1, 1), every, pl.ds(1, 1), mid, (me_ax + 1, me_az)),
-          halo(1, pl.ds(nx - 2, 1), every, pl.ds(0, 1), mid, (me_ax + 1, me_az))]
-    down = [halo(2, pl.ds(0, 1), every, pl.ds(nx + 2, 1), mid, (me_ax - 1, me_az)),
-            halo(3, pl.ds(1, 1), every, pl.ds(nx + 3, 1), mid, (me_ax - 1, me_az))]
-    around = halo(4, pl.ds(0, nx), pl.ds(nt - SUB, SUB), pl.ds(2, nx), pl.ds(EDGE - SUB, SUB), (me_ax, right))
-    around += halo(5, pl.ds(0, nx), pl.ds(0, SUB), pl.ds(2, nx), pl.ds(EDGE + nt, SUB), (me_ax, left))
-
-    for c in around:
-        c.start()
-    for step in range(2):
+    def planes(kind, src, dst, target):
+        def cells(at, rows, first, count):
+            return halo(kind + at, pl.ds(src + rows[0], rows[1]), pl.ds(first, count),
+                        pl.ds(dst + rows[0], rows[1]), pl.ds(EDGE + first, count), target)
+
+        near_row = nx - 1 - src if src else 0
+        inner = nt - 2 * SUB
+        return (
+            cells(0, (0, 2), 0, SUB) + cells(1, (0, 2), nt - SUB, SUB),
+            cells(2, (near_row, 1), SUB, inner),
+            cells(3, (1 - near_row, 1), SUB, inner),
+        )
+
+    up = planes(0, nx - 2, 0, (me_ax + 1, me_az))
+    down = planes(4, 0, nx + 2, (me_ax - 1, me_az))
+    around = halo(8, pl.ds(0, nx), pl.ds(nt - SUB, SUB), pl.ds(2, nx), pl.ds(EDGE - SUB, SUB), (me_ax, right))
+    around += halo(9, pl.ds(0, nx), pl.ds(0, SUB), pl.ds(2, nx), pl.ds(EDGE + nt, SUB), (me_ax, left))
+
+    for step in range(3):
         @pl.when(has_hi)
         def _():
             for c in up[step]:
@@ -159,46 +167,41 @@
             for c in down[step]:
                 c.start()
 
+        if step == 0:
+            for c in around:
+                c.start()
+
     def corner(slot, row):
+        rows = pl.ds(row, 2)
         return [
             pltpu.make_async_remote_copy(
-                src_ref=S.at[:, row, :, pl.ds(EDGE + nt - SUB, SUB), :],
-                dst_ref=S.at[:, row, :, pl.ds(EDGE - SUB, SUB), :],
+                src_ref=S.at[:, rows, :, pl.ds(EDGE + nt - SUB, SUB), :],
+                dst_ref=S.at[:, rows, :, pl.ds(EDGE - SUB, SUB), :],
                 send_sem=corner_send.at[slot, 0], recv_sem=corner_recv.at[slot, 0],
                 device_id=(me_ax, right), device_id_type=MESH_ID),
             pltpu.make_async_remote_copy(
-                src_ref=S.at[:, row, :, pl.ds(EDGE, SUB), :],
-                dst_ref=S.at[:, row, :, pl.ds(EDGE + nt, SUB), :],
+                src_ref=S.at[:, rows, :, pl.ds(EDGE, SUB), :],
+                dst_ref=S.at[:, rows, :, pl.ds(EDGE + nt, SUB), :],
                 send_sem=corner_send.at[slot, 1], recv_sem=corner_recv.at[slot, 1],
                 device_id=(me_ax, left), device_id_type=MESH_ID),
         ]
 
+    lo_corner, hi_corner = corner(0, 0), corner(1, nx + 2)
+
     def receive(step):
-        lo_corner, hi_corner = corner(step, 1 - step), corner(2 + step, nx + 2 + step)
-
         @pl.when(has_lo)
         def _():
             for c in up[step]:
                 c.wait_recv()
             for c in lo_corner:
-                c.start()
+                c.start() if step == 0 else c.wait() if step == 1 else None
 
         @pl.when(has_hi)
         def _():
             for c in down[step]:
                 c.wait_recv()
             for c in hi_corner:
-                c.start()
-
-        @pl.when(has_lo)
-        def _():
-            for c in lo_corner:
-                c.wait()
-
-        @pl.when(has_hi)
-        def _():
-            for c in hi_corner:
-                c.wait()
+                c.start() if step == 0 else c.wait() if step == 1 else None
 
     def low(r):
         return jnp.maximum(r - 1, jnp.where(has_lo, -2, 0))
@@ -207,6 +210,8 @@
         return jnp.minimum(r + 1, jnp.where(has_hi, nx + 1, nx - 1))
 
     def sweep(first, stride, count, tiles, body):
+        tiles = tiles // body.size
+
         def step(at, carry):
             r = first + stride * (at // tiles)
             body(r, lax.rem(at, tiles))
@@ -216,25 +221,40 @@
 
     wide = nt // SUB + 2
 
-    def near(ref, lead, row, col, shift):
-        return ref[lead, row, :, pl.ds(col + shift, SUB), :]
-
-    def tile(ref, lead, row, col):
-        return ref[lead, row, :, pl.ds(pl.multiple_of(col, SUB), SUB), :]
+    def blocked(name, extent):
+        size = math.gcd(BLOCKS[name], extent)
+
+        def mark(body):
+            body.size = size
+            return body
+
+        return size * SUB, mark
+
+    def spread(values, rows):
+        return jnp.concatenate([values] * (rows // SUB), axis=1)
+
+    def near(ref, lead, row, col, shift, n):
+        return ref[lead, row, :, pl.ds(col + shift, n), :]
+
+    def tile(ref, lead, row, col, n):
+        return ref[lead, row, :, pl.ds(pl.multiple_of(col, SUB), n), :]
 
     def put(ref, lead, row, col, value):
-        ref[lead, row, :, pl.ds(pl.multiple_of(col, SUB), SUB), :] = value
+        ref[lead, row, :, pl.ds(pl.multiple_of(col, SUB), value.shape[1]), :] = value
 
     def first_pass(with_pairs):
+        n, mark = blocked("first", wide)
+
+        @mark
         def body(r, t):
-            c = (EDGE - SUB) + t * SUB
+            c = (EDGE - SUB) + t * n
             rows = (low(r) + 2, r + 2, high(r) + 2)
-            rho = [tile(S, 0, q, c) for q in rows]
-            vel = [[tile(S, 1 + a, q, c) for a in range(3)] for q in rows]
-            inv_r, az_scale, width = geo_ref[0], geo_ref[1], geo_ref[2]
+            rho = [tile(S, 0, q, c, n) for q in rows]
+            vel = [[tile(S, 1 + a, q, c, n) for a in range(3)] for q in rows]
+            inv_r, az_scale, width = (spread(geo_ref[g], n) for g in (0, 1, 2))
             dx = [vel[2][a] - vel[0][a] for a in range(3)]
             dr = [rise(vel[1][a]) * (0.5 / STEP_RADIAL) for a in range(3)]
-            dt = [(near(S, 1 + a, r + 2, c, 1) - near(S, 1 + a, r + 2, c, -1)) * az_scale for a in range(3)]
+            dt = [(near(S, 1 + a, r + 2, c, 1, n) - near(S, 1 + a, r + 2, c, -1, n)) * az_scale for a in range(3)]
             dev, size = strain(dx, dr, dt, vel[1][1], vel[1][2], inv_r)
             scale = rho[1] * width * size
             for a in range(6):
@@ -249,44 +269,57 @@
                     put(PX, at, r, c, (p[0] + p[1]) + (p[1] + p[2]))
         return body
 
-    def smooth(ref, lead, row, c):
-        mid_value = tile(ref, lead, row, c)
-        s = (near(ref, lead, row, c, -1) + near(ref, lead, row, c, 1)) + (mid_value + mid_value)
+    def smooth(ref, lead, row, c, n):
+        mid_value = tile(ref, lead, row, c, n)
+        s = (near(ref, lead, row, c, -1, n) + near(ref, lead, row, c, 1, n)) + (mid_value + mid_value)
         return ((before(s) + after(s)) + (s + s)) * (1.0 / 64.0)
 
+    n_hat, mark_hat = blocked("hat", wide)
+
+    @mark_hat
     def hat_pass(r, t):
-        c = (EDGE - SUB) + t * SUB
-        hat = [smooth(H, a, r + 1, c) for a in range(4)]
+        n = n_hat
+        c = (EDGE - SUB) + t * n
+        hat = [smooth(H, a, r + 1, c, n) for a in range(4)]
         inv = 1.0 / hat[0]
         for a in range(4):
             put(HM, a, r + 1, c, hat[a])
         for a in range(3):
             put(V, a, r + 1, c, hat[1 + a] * inv)
 
+    n_model, mark_model = blocked("model", wide)
+
+    @mark_model
     def model_pass(r, t):
-        c = (EDGE - SUB) + t * SUB
+        n = n_model
+        c = (EDGE - SUB) + t * n
         for a in range(6):
-            m = tile(M, a, r + 1, c)
-            put(MX, a, r, c, (tile(M, a, low(r) + 1, c) + m) + (m + tile(M, a, high(r) + 1, c)))
-
+            m = tile(M, a, r + 1, c, n)
+            put(MX, a, r, c, (tile(M, a, low(r) + 1, c, n) + m) + (m + tile(M, a, high(r) + 1, c, n)))
+
+    n_closure, mark_closure = blocked("closure", nt // SUB)
+
+    @mark_closure
     def closure_pass(r, t):
-        c = EDGE + t * SUB
-        inv_r, az_scale, width4 = geo_ref[0], geo_ref[1], geo_ref[3]
-        hv = [tile(V, a, r + 1, c) for a in range(3)]
-        dx = [tile(V, a, high(r) + 1, c) - tile(V, a, low(r) + 1, c) for a in range(3)]
+        n = n_closure
+        c = EDGE + t * n
+        inv_r, az_scale, width4 = (spread(geo_ref[g], n) for g in (0, 1, 3))
+        hv = [tile(V, a, r + 1, c, n) for a in range(3)]
+        dx = [tile(V, a, high(r) + 1, c, n) - tile(V, a, low(r) + 1, c, n) for a in range(3)]
         dr = [rise(hv[a]) * (0.5 / STEP_RADIAL) for a in range(3)]
-        dt = [(near(V, a, r + 1, c, 1) - near(V, a, r + 1, c, -1)) * az_scale for a in range(3)]
+        dt = [(near(V, a, r + 1, c, 1, n) - near(V, a, r + 1, c, -1, n)) * az_scale for a in range(3)]
         dev, size = strain(dx, dr, dt, hv[1], hv[2], inv_r)
-        scale = width4 * tile(HM, 0, r + 1, c) * size
-        hm = [tile(HM, 1 + a, r + 1, c) for a in range(3)]
+        scale = width4 * tile(HM, 0, r + 1, c, n) * size
+        hm = [tile(HM, 1 + a, r + 1, c, n) for a in range(3)]
         lm, mm = [], []
         for at, (a, b) in enumerate(PAIRS):
-            mixed = scale * dev[at] - smooth(MX, at, r, c)
-            leonard = smooth(PX, at, r, c) - hm[a] * hv[b]
+            mixed = scale * dev[at] - smooth(MX, at, r, c, n)
+            leonard = smooth(PX, at, r, c, n) - hm[a] * hv[b]
             lm.append(leonard * mixed)
             mm.append(mixed * mixed)
-        ACC[r, 0] += (lm[0] + lm[1] + lm[2]) + 2.0 * (lm[3] + lm[4] + lm[5])
-        ACC[r, 1] += (mm[0] + mm[1] + mm[2]) + 2.0 * (mm[3] + mm[4] + mm[5])
+        for q, terms in enumerate((lm, mm)):
+            cells = (terms[0] + terms[1] + terms[2]) + 2.0 * (terms[3] + terms[4] + terms[5])
+            ACC[r, q] += sum(cells[:, s:s + SUB] for s in range(0, n, SUB))
 
     ACC[...] = jnp.zeros_like(ACC)
     for c in own:
@@ -296,11 +329,12 @@
     sweep(1, 1, nx - 2, wide, first_pass(True))
     sweep(1, 1, nx - 2, wide, hat_pass)
     receive(0)
+    receive(1)
     sweep(0, nx - 1, 2, wide, first_pass(True))
     sweep(0, nx - 1, 2, wide, hat_pass)
     sweep(1, 1, nx - 2, wide, model_pass)
     sweep(1, 1, nx - 2, nt // SUB, closure_pass)
-    receive(1)
+    receive(2)
     sweep(-1, nx + 1, 2, wide, first_pass(False))
     sweep(-1, nx + 1, 2, wide, hat_pass)
     sweep(0, nx - 1, 2, wide, model_pass)
@@ -358,30 +392,33 @@
         for h in range(nh):
             coef_ref[pl.ds(r, 1), pl.ds(h * LANES, LANES)] = value[h:h + 1]
 
+    n_flux, mark_flux = blocked("flux", nt // SUB)
+
+    @mark_flux
     def flux_pass(r, t):
-        c = EDGE + t * SUB
-        inv_r, az_scale = geo_ref[0], geo_ref[1]
-        radius, back, radius2, back2 = geo_ref[4], geo_ref[5], geo_ref[6], geo_ref[7]
+        n = n_flux
+        c = EDGE + t * n
+        inv_r, az_scale, radius, back, radius2, back2 = (spread(geo_ref[g], n) for g in (0, 1, 4, 5, 6, 7))
         lo, hi = low(r) + 1, high(r) + 1
-        here, below, above = CS[r + 1], CS[lo], CS[hi]
+        here, below, above = (spread(CS[q], n) for q in (r + 1, lo, hi))
 
         def axial(a):
-            return above * tile(M, a, hi, c) - below * tile(M, a, lo, c)
+            return above * tile(M, a, hi, c, n) - below * tile(M, a, lo, c, n)
 
         def around_of(a):
-            return (near(M, a, r + 1, c, 1) - near(M, a, r + 1, c, -1)) * turn
+            return (near(M, a, r + 1, c, 1, n) - near(M, a, r + 1, c, -1, n)) * turn
 
         turn = here * az_scale
         once = here * radius
-        d_xr = rise(once * tile(M, 3, r + 1, c)) * back
-        d_rr = rise(once * tile(M, 1, r + 1, c)) * back
-        d_rt = rise(here * radius2 * tile(M, 5, r + 1, c)) * back2
+        d_xr = rise(once * tile(M, 3, r + 1, c, n)) * back
+        d_rr = rise(once * tile(M, 1, r + 1, c, n)) * back
+        d_rt = rise(here * radius2 * tile(M, 5, r + 1, c, n)) * back2
         out = (
             axial(0) + d_xr + around_of(4),
-            axial(3) + d_rr + around_of(5) - here * tile(M, 2, r + 1, c) * inv_r,
+            axial(3) + d_rr + around_of(5) - here * tile(M, 2, r + 1, c, n) * inv_r,
             axial(4) + d_rt + around_of(2),
         )
-        rows = pl.ds(pl.multiple_of(t * SUB, SUB), SUB)
+        rows = pl.ds(pl.multiple_of(t * n, SUB), n)
         for a in range(3):
             for h in range(nh):
                 flux_ref[a, r, rows, pl.ds(h * LANES, LANES)] = out[a][h]
@@ -407,13 +444,28 @@
 
     @pl.when(has_hi)
     def _():
-        for c in up[0] + up[1] + to_hi:
+        for c in up[0] + up[1] + up[2] + to_hi:
             c.wait_send()
 
     @pl.when(has_lo)
     def _():
-        for c in down[0] + down[1] + to_lo:
+        for c in down[0] + down[1] + down[2] + to_lo:
             c.wait_send()
+
+
+def hand_over(flux_in, coef_in, flux_out, coef_out, flux_buf, coef_buf, sems):
+    count = flux_in.shape[0]
+    pieces = [(flux_in.at[a], flux_buf.at[a], flux_out.at[a]) for a in range(count)]
+    pieces.append((coef_in, coef_buf, coef_out))
+    take = [pltpu.make_async_copy(a, b, sems.at[0, at]) for at, (a, b, _) in enumerate(pieces)]
+    give = [pltpu.make_async_copy(b, c, sems.at[1, at]) for at, (_, b, c) in enumerate(pieces)]
+    for c in take:
+        c.start()
+    for arrive, leave in zip(take, give):
+        arrive.wait()
+        leave.start()
+    for c in give:
+        c.wait()
 
 
 def shards(n_ax, n_az, density, velocity):
@@ -426,7 +478,7 @@
         return pltpu.VMEM((count, rows, nh, cols, LANES), jnp.float32)
 
     dma = pltpu.SemaphoreType.DMA
-    return pl.pallas_call(
+    flux, coef = pl.pallas_call(
         functools.partial(kernel, n_ax, n_az, nx, nt, nh),
         out_shape=(
             jax.ShapeDtypeStruct(velocity.shape, jnp.float32),
@@ -456,16 +508,32 @@
             pltpu.VMEM((n_az, 2 * nh, LANES), jnp.float32),
             pltpu.VMEM((nx + 2, nh, SUB, LANES), jnp.float32),
             dma((2 * nh,)),
-            dma((6, 2 * nh)),
-            dma((6, 2 * nh)),
-            dma((4, 2)),
-            dma((4, 2)),
+            dma((10, 2 * nh)),
+            dma((10, 2 * nh)),
+            dma((2, 2)),
+            dma((2, 2)),
             dma((3, n_az)),
             dma((3, n_az)),
         ],
         compiler_params=pltpu.CompilerParams(collective_id=0, has_side_effects=True),
         name="closure",
     )(density, velocity, geo)
+    anywhere = pl.BlockSpec(memory_space=pl.ANY)
+    return pl.pallas_call(
+        hand_over,
+        out_shape=(
+            jax.ShapeDtypeStruct(flux.shape, jnp.float32),
+            jax.ShapeDtypeStruct(coef.shape, jnp.float32),
+        ),
+        in_specs=[anywhere, anywhere],
+        out_specs=(anywhere, anywhere),
+        scratch_shapes=[
+            pltpu.VMEM(flux.shape, jnp.float32),
+            pltpu.VMEM(coef.shape, jnp.float32),
+            dma((2, flux.shape[0] + 1)),
+        ],
+        name="hand_over",
+    )(flux, coef)
 
 
 def solution(mesh):

time: 54 us -> 40.2 us (0.74)
  Pallas kernels: 50.5 us -> 39.4 us
  local copies, waits for them, and re-layouts: 2.66 us -> 0 us
    pallas_call x1, Pallas kernels: 50.5 us -> 37.5 us  [shards(): pl.pallas_call(functools.partial(kernel, n_ax, n_az, nx, nt, nh), out_sha...]
    unnamed x4 -> x0, local copies, waits for them, and re-layouts: 2.66 us -> none
    pallas_call x0 -> x1, Pallas kernels: none -> 1.9 us  [shards(): pl.pallas_call(hand_over, out_shape=(jax.ShapeDtypeStruct(flux.shape, jnp...]
where the time goes in v2:
time: 40.2 us; the launch traced here: 40 us
  Pallas kernels  39.4 us (98%)
  between operations  0.64 us (2%)
    pallas_call x1, Pallas kernels, shards(): pl.pallas_call(functools.partial(kernel, n_ax, n_az, nx, nt, nh), out_sha...  37.5 us
    pallas_call x1, Pallas kernels, shards(): pl.pallas_call(hand_over, out_shape=(jax.ShapeDtypeStruct(flux.shape, jnp...  1.9 us

profile of v2, /device:TPU:0, one launch (start us, length us, event | category | flops | bytes accessed | tf_op | source)
XLA Modules:
  0.0 40.0 jit_solution(14936567051253961922)
XLA Ops:
  0.6 37.5 %closure.1 = (f32[3,4,64,256]{3,2,1,0:T(8,128)}, f32[4,256]{1,0:T(4,128)}) custom-call(f32[4,64,256]{2,1,0:T(8,128)} %rho_ref.1, f32[3,4,64,256]{3,2,1,0:T(8,128)} %vel_ref.1, f32[8,2,8,128]{3,2,1,0:T(8,128)} %constant.2.clone.geo_ref), custom_call_target="tpu_custom_call" | custom-call | tf_op jit(solution)/shard_map/closure/pallas_call | solution.py:481
  38.1 1.9 %hand_over.1 = (f32[3,4,64,256]{3,2,1,0:T(8,128)}, f32[4,256]{1,0:T(4,128)}) custom-call(f32[3,4,64,256]{3,2,1,0:T(8,128)} %get-tuple-element.4.flux_in, f32[4,256]{1,0:T(4,128)} %get-tuple-element.5.coef_in), custom_call_target="tpu_custom_call" | custom-call | tf_op jit(solution)/shard_map/hand_over/pallas_call | solution.py:522

commit v3 on v2

--- a/solution.py
+++ b/solution.py
@@ -80,10 +80,11 @@
 
 
 def kernel(
-    n_ax, n_az, nx, nt, nh,
+    n_ax, n_az, nx, nt, nh, relays,
     rho_ref, vel_ref, geo_ref, flux_ref, coef_ref,
-    S, M, H, V, HM, PX, MX, ACC, part, rec, rec_lo, rec_hi, CS,
+    S, M, H, V, HM, PX, MX, ACC, part, rec, rec_lo, rec_hi, CS, R,
     own_sem, halo_send, halo_recv, corner_send, corner_recv, sum_send, sum_recv,
+    relay_send, relay_recv, pass_send,
 ):
     me_ax, me_az = lax.axis_index("ax"), lax.axis_index("az")
     left, right = lax.rem(me_az + n_az - 1, n_az), lax.rem(me_az + 1, n_az)
@@ -120,6 +121,16 @@
             greet(me_ax + 1, lax.rem(me_az + d, n_az))
 
     peers = n_az - 1 + jnp.where(has_lo, n_az, 0) + jnp.where(has_hi, n_az, 0)
+    if relays:
+        @pl.when(me_ax > 1)
+        def _():
+            greet(me_ax - 2, me_az)
+
+        @pl.when(me_ax < n_ax - 2)
+        def _():
+            greet(me_ax + 2, me_az)
+
+        peers = peers + jnp.where(me_ax > 1, 1, 0) + jnp.where(me_ax < n_ax - 2, 1, 0)
     pl.semaphore_wait(barrier, peers)
 
     def halo(kind, src_rows, src_cols, dst_rows, dst_cols, target):
@@ -144,31 +155,95 @@
                         pl.ds(dst + rows[0], rows[1]), pl.ds(EDGE + first, count), target)
 
         near_row = nx - 1 - src if src else 0
-        inner = nt - 2 * SUB
         return (
             cells(0, (0, 2), 0, SUB) + cells(1, (0, 2), nt - SUB, SUB),
-            cells(2, (near_row, 1), SUB, inner),
-            cells(3, (1 - near_row, 1), SUB, inner),
+            cells(2, (near_row, 1), SUB, span),
+            cells(3, (near_row, 1), SUB + span, span),
+            cells(4, (1 - near_row, 1), SUB, span),
+            cells(5, (1 - near_row, 1), SUB + span, span),
         )
 
+    span = nt // 2 - SUB
     up = planes(0, nx - 2, 0, (me_ax + 1, me_az))
-    down = planes(4, 0, nx + 2, (me_ax - 1, me_az))
-    around = halo(8, pl.ds(0, nx), pl.ds(nt - SUB, SUB), pl.ds(2, nx), pl.ds(EDGE - SUB, SUB), (me_ax, right))
-    around += halo(9, pl.ds(0, nx), pl.ds(0, SUB), pl.ds(2, nx), pl.ds(EDGE + nt, SUB), (me_ax, left))
-
-    for step in range(3):
-        @pl.when(has_hi)
-        def _():
-            for c in up[step]:
+    down = planes(6, 0, nx + 2, (me_ax - 1, me_az))
+    around = halo(12, pl.ds(0, nx), pl.ds(nt - SUB, SUB), pl.ds(2, nx), pl.ds(EDGE - SUB, SUB), (me_ax, right))
+    around += halo(13, pl.ds(0, nx), pl.ds(0, SUB), pl.ds(2, nx), pl.ds(EDGE + nt, SUB), (me_ax, left))
+
+    pair, odd = me_ax // 2, lax.rem(me_ax, 2)
+    is_odd, is_even = odd == 1, odd == 0
+    rank_of = {5: 0, 4: 1, 3: 2}
+    sent = jnp.where(is_odd, n_ax // 2 - 1 - pair, pair)
+    passed = jnp.where(is_odd, pair, n_ax // 2 - 1 - pair)
+
+    def relay(piece):
+        rank, copies = rank_of[piece], []
+        row = jnp.where(is_odd, nx - 1, 0) if piece == 3 else jnp.where(is_odd, nx - 2, 1)
+        first = SUB + (0 if piece == 4 else span)
+        to = (me_ax + 1 - 2 * odd, me_az)
+        on = (me_ax + 2 - 4 * odd, me_az)
+        land = jnp.where(is_odd, nx + 2, 1) if piece == 3 else jnp.where(is_odd, nx + 3, 0)
+        kind = piece + 6 * odd
+        onward = []
+        for h in range(nh):
+            lanes = pl.ds(h * LANES, LANES)
+            for q, src, lead in (
+                (2 * h, rho_ref.at[pl.ds(row, 1), pl.ds(first, span), lanes], 0),
+                (2 * h + 1, vel_ref.at[:, pl.ds(row, 1), pl.ds(first, span), lanes], pl.ds(1, 3)),
+            ):
+                copies.append(pltpu.make_async_remote_copy(
+                    src_ref=src, dst_ref=R.at[rank, lead, :, h],
+                    send_sem=relay_send.at[rank, q], recv_sem=relay_recv.at[rank, q],
+                    device_id=to, device_id_type=MESH_ID))
+                onward.append(pltpu.make_async_remote_copy(
+                    src_ref=R.at[rank, lead, :, h],
+                    dst_ref=S.at[lead, pl.ds(land, 1), h, pl.ds(EDGE + first, span), :],
+                    send_sem=pass_send.at[rank, q], recv_sem=halo_recv.at[kind, q],
+                    device_id=on, device_id_type=MESH_ID))
+        return copies, onward
+
+    relayed = {piece: relay(piece) for piece in rank_of} if relays else {}
+
+    def sends_up(piece):
+        return has_hi & (is_even | (sent <= rank_of[piece])) if piece in relayed else has_hi
+
+    def sends_down(piece):
+        return has_lo & (is_odd | (sent <= rank_of[piece])) if piece in relayed else has_lo
+
+    def send_relay(piece):
+        if piece in relayed:
+            @pl.when(sent > rank_of[piece])
+            def _():
+                for c in relayed[piece][0]:
+                    c.start()
+
+    def pass_on(piece):
+        if piece in relayed:
+            @pl.when(passed > rank_of[piece])
+            def _():
+                for got, c in zip(*relayed[piece]):
+                    got.wait_recv()
+                    c.start()
+
+    for piece in range(5 + 1):
+        at = max(piece - 1, 0)
+        if piece == 1:
+            for c in around:
                 c.start()
-
-        @pl.when(has_lo)
-        def _():
-            for c in down[step]:
+            continue
+        if piece == 3:
+            send_relay(3)
+        if piece == 4:
+            send_relay(4)
+            send_relay(5)
+
+        @pl.when(sends_up(piece))
+        def _():
+            for c in up[at]:
                 c.start()
 
-        if step == 0:
-            for c in around:
+        @pl.when(sends_down(piece))
+        def _():
+            for c in down[at]:
                 c.start()
 
     def corner(slot, row):
@@ -188,17 +263,20 @@
 
     lo_corner, hi_corner = corner(0, 0), corner(1, nx + 2)
 
+    def groups(flow):
+        return flow[0], flow[1] + flow[2], flow[3] + flow[4]
+
     def receive(step):
         @pl.when(has_lo)
         def _():
-            for c in up[step]:
+            for c in groups(up)[step]:
                 c.wait_recv()
             for c in lo_corner:
                 c.start() if step == 0 else c.wait() if step == 1 else None
 
         @pl.when(has_hi)
         def _():
-            for c in down[step]:
+            for c in groups(down)[step]:
                 c.wait_recv()
             for c in hi_corner:
                 c.start() if step == 0 else c.wait() if step == 1 else None
@@ -329,9 +407,12 @@
     sweep(1, 1, nx - 2, wide, first_pass(True))
     sweep(1, 1, nx - 2, wide, hat_pass)
     receive(0)
+    pass_on(3)
     receive(1)
+    pass_on(4)
     sweep(0, nx - 1, 2, wide, first_pass(True))
     sweep(0, nx - 1, 2, wide, hat_pass)
+    pass_on(5)
     sweep(1, 1, nx - 2, wide, model_pass)
     sweep(1, 1, nx - 2, nt // SUB, closure_pass)
     receive(2)
@@ -442,14 +523,38 @@
     for c in across + around:
         c.wait_send()
 
+    for piece in (0, 2, 3, 4, 5):
+        at = max(piece - 1, 0)
+
+        @pl.when(sends_up(piece))
+        def _():
+            for c in up[at]:
+                c.wait_send()
+
+        @pl.when(sends_down(piece))
+        def _():
+            for c in down[at]:
+                c.wait_send()
+
+    for piece, (copies, onward) in relayed.items():
+        @pl.when(sent > rank_of[piece])
+        def _():
+            for c in copies:
+                c.wait_send()
+
+        @pl.when(passed > rank_of[piece])
+        def _():
+            for c in onward:
+                c.wait_send()
+
     @pl.when(has_hi)
     def _():
-        for c in up[0] + up[1] + up[2] + to_hi:
+        for c in to_hi:
             c.wait_send()
 
     @pl.when(has_lo)
     def _():
-        for c in down[0] + down[1] + down[2] + to_lo:
+        for c in to_lo:
             c.wait_send()
 
 
@@ -472,6 +577,7 @@
     nx, nt, radial = density.shape
     nh = radial // LANES
     cols = nt + 2 * EDGE
+    relays = n_ax == 8
     geo = jnp.asarray(geometry(radial, nt * n_az))
 
     def field(count, rows):
@@ -479,7 +585,7 @@
 
     dma = pltpu.SemaphoreType.DMA
     flux, coef = pl.pallas_call(
-        functools.partial(kernel, n_ax, n_az, nx, nt, nh),
+        functools.partial(kernel, n_ax, n_az, nx, nt, nh, relays),
         out_shape=(
             jax.ShapeDtypeStruct(velocity.shape, jnp.float32),
             jax.ShapeDtypeStruct((nx, radial), jnp.float32),
@@ -507,13 +613,17 @@
             pltpu.VMEM((n_az, 2 * nh, LANES), jnp.float32),
             pltpu.VMEM((n_az, 2 * nh, LANES), jnp.float32),
             pltpu.VMEM((nx + 2, nh, SUB, LANES), jnp.float32),
+            pltpu.VMEM((3, 4, 1, nh, nt // 2 - SUB, LANES), jnp.float32),
             dma((2 * nh,)),
-            dma((10, 2 * nh)),
-            dma((10, 2 * nh)),
+            dma((14, 2 * nh)),
+            dma((14, 2 * nh)),
             dma((2, 2)),
             dma((2, 2)),
             dma((3, n_az)),
             dma((3, n_az)),
+            dma((3, 2 * nh)),
+            dma((3, 2 * nh)),
+            dma((3, 2 * nh)),
         ],
         compiler_params=pltpu.CompilerParams(collective_id=0, has_side_effects=True),
         name="closure",

time: 40.2 us -> 39 us (0.970)
  Pallas kernels: 39.4 us -> 38.2 us
    pallas_call x1, Pallas kernels: 37.5 us -> 36.3 us  [shards(): pl.pallas_call(functools.partial(kernel, n_ax, n_az, nx, nt, nh, relays),...]
where the time goes in v3:
time: 39 us; the launch traced here: 38.8 us
  Pallas kernels  38.2 us (98%)
  between operations  0.64 us (2%)
    pallas_call x1, Pallas kernels, shards(): pl.pallas_call(functools.partial(kernel, n_ax, n_az, nx, nt, nh, relays),...  36.3 us
    pallas_call x1, Pallas kernels, shards(): pl.pallas_call(hand_over, out_shape=(jax.ShapeDtypeStruct(flux.shape, jnp...  1.9 us

profile of v3, /device:TPU:0, one launch (start us, length us, event | category | flops | bytes accessed | tf_op | source)
XLA Modules:
  0.0 38.8 jit_solution(7282433283618690979)
XLA Ops:
  0.6 36.3 %closure.1 = (f32[3,4,64,256]{3,2,1,0:T(8,128)}, f32[4,256]{1,0:T(4,128)}) custom-call(f32[4,64,256]{2,1,0:T(8,128)} %rho_ref.1, f32[3,4,64,256]{3,2,1,0:T(8,128)} %vel_ref.1, f32[8,2,8,128]{3,2,1,0:T(8,128)} %constant.2.clone.geo_ref), custom_call_target="tpu_custom_call" | custom-call | tf_op jit(solution)/shard_map/closure/pallas_call | solution.py:587
  36.9 1.9 %hand_over.1 = (f32[3,4,64,256]{3,2,1,0:T(8,128)}, f32[4,256]{1,0:T(4,128)}) custom-call(f32[3,4,64,256]{3,2,1,0:T(8,128)} %get-tuple-element.4.flux_in, f32[4,256]{1,0:T(4,128)} %get-tuple-element.5.coef_in), custom_call_target="tpu_custom_call" | custom-call | tf_op jit(solution)/shard_map/hand_over/pallas_call | solution.py:632

commit v4 on v3

--- a/solution.py
+++ b/solution.py
@@ -17,7 +17,7 @@
 PAIRS = ((0, 0), (1, 1), (2, 2), (0, 1), (0, 2), (1, 2))
 LANES = 128
 SUB = 8
-BLOCKS = {"first": 5, "hat": 10, "model": 10, "closure": 4, "flux": 4}
+BLOCKS = {"first": 10, "hat": 10, "model": 10, "closure": 8, "flux": 8}
 EDGE = 16
 MESH_ID = pl.DeviceIdType.MESH
 
@@ -82,7 +82,7 @@
 def kernel(
     n_ax, n_az, nx, nt, nh, relays,
     rho_ref, vel_ref, geo_ref, flux_ref, coef_ref,
-    S, M, H, V, HM, PX, MX, ACC, part, rec, rec_lo, rec_hi, CS, R,
+    S, M, H, V, HM, PX, MX, ACC, part, rec, rec_lo, rec_hi, CS, R, LE,
     own_sem, halo_send, halo_recv, corner_send, corner_recv, sum_send, sum_recv,
     relay_send, relay_recv, pass_send,
 ):
@@ -375,6 +375,17 @@
             m = tile(M, a, r + 1, c, n)
             put(MX, a, r, c, (tile(M, a, low(r) + 1, c, n) + m) + (m + tile(M, a, high(r) + 1, c, n)))
 
+    n_leonard, mark_leonard = blocked("closure", nt // SUB)
+
+    @mark_leonard
+    def leonard_pass(r, t):
+        n = n_leonard
+        c = EDGE + t * n
+        hv = [tile(V, a, r + 1, c, n) for a in range(3)]
+        hm = [tile(HM, 1 + a, r + 1, c, n) for a in range(3)]
+        for at, (a, b) in enumerate(PAIRS):
+            put(LE, at, r, c, smooth(PX, at, r, c, n) - hm[a] * hv[b])
+
     n_closure, mark_closure = blocked("closure", nt // SUB)
 
     @mark_closure
@@ -388,11 +399,10 @@
         dt = [(near(V, a, r + 1, c, 1, n) - near(V, a, r + 1, c, -1, n)) * az_scale for a in range(3)]
         dev, size = strain(dx, dr, dt, hv[1], hv[2], inv_r)
         scale = width4 * tile(HM, 0, r + 1, c, n) * size
-        hm = [tile(HM, 1 + a, r + 1, c, n) for a in range(3)]
         lm, mm = [], []
-        for at, (a, b) in enumerate(PAIRS):
+        for at in range(6):
             mixed = scale * dev[at] - smooth(MX, at, r, c, n)
-            leonard = smooth(PX, at, r, c, n) - hm[a] * hv[b]
+            leonard = tile(LE, at, r, c, n)
             lm.append(leonard * mixed)
             mm.append(mixed * mixed)
         for q, terms in enumerate((lm, mm)):
@@ -413,6 +423,7 @@
     sweep(0, nx - 1, 2, wide, first_pass(True))
     sweep(0, nx - 1, 2, wide, hat_pass)
     pass_on(5)
+    sweep(0, 1, nx, nt // SUB, leonard_pass)
     sweep(1, 1, nx - 2, wide, model_pass)
     sweep(1, 1, nx - 2, nt // SUB, closure_pass)
     receive(2)
@@ -614,6 +625,7 @@
             pltpu.VMEM((n_az, 2 * nh, LANES), jnp.float32),
             pltpu.VMEM((nx + 2, nh, SUB, LANES), jnp.float32),
             pltpu.VMEM((3, 4, 1, nh, nt // 2 - SUB, LANES), jnp.float32),
+            field(6, nx),
             dma((2 * nh,)),
             dma((14, 2 * nh)),
             dma((14, 2 * nh)),

time: 39 us -> 38.2 us (0.979)
  Pallas kernels: 38.2 us -> 37.3 us
    pallas_call x1, Pallas kernels: 36.3 us -> 35.4 us  [shards(): pl.pallas_call(functools.partial(kernel, n_ax, n_az, nx, nt, nh, relays),...]
where the time goes in v4:
time: 38.2 us; the launch traced here: 38 us
  Pallas kernels  37.3 us (98%)
  between operations  0.64 us (2%)
    pallas_call x1, Pallas kernels, shards(): pl.pallas_call(functools.partial(kernel, n_ax, n_az, nx, nt, nh, relays),...  35.4 us
    pallas_call x1, Pallas kernels, shards(): pl.pallas_call(hand_over, out_shape=(jax.ShapeDtypeStruct(flux.shape, jnp...  1.9 us

profile of v4, /device:TPU:0, one launch (start us, length us, event | category | flops | bytes accessed | tf_op | source)
XLA Modules:
  0.0 38.0 jit_solution(14557352238024562336)
XLA Ops:
  0.6 35.4 %closure.1 = (f32[3,4,64,256]{3,2,1,0:T(8,128)}, f32[4,256]{1,0:T(4,128)}) custom-call(f32[4,64,256]{2,1,0:T(8,128)} %rho_ref.1, f32[3,4,64,256]{3,2,1,0:T(8,128)} %vel_ref.1, f32[8,2,8,128]{3,2,1,0:T(8,128)} %constant.2.clone.geo_ref), custom_call_target="tpu_custom_call" | custom-call | tf_op jit(solution)/shard_map/closure/pallas_call | solution.py:598
  36.1 1.9 %hand_over.1 = (f32[3,4,64,256]{3,2,1,0:T(8,128)}, f32[4,256]{1,0:T(4,128)}) custom-call(f32[3,4,64,256]{3,2,1,0:T(8,128)} %get-tuple-element.4.flux_in, f32[4,256]{1,0:T(4,128)} %get-tuple-element.5.coef_in), custom_call_target="tpu_custom_call" | custom-call | tf_op jit(solution)/shard_map/hand_over/pallas_call | solution.py:644
